TPU v7x, 32 devices: a whole 2x2x4 slice. The times are simulated.
32 devices in a mesh: expert: 16 (over z, y, x), mp: 2 (over core).
Axes of the slice: x: 2, y: 2, z: 4, core: 2. Of those that a mesh axis runs over, the one named last changes fastest.
Arguments:
- tokens: bfloat16 [256, 4096], P('expert'), may hold values from -8 to 8
- norm_gain: bfloat16 [4096], replicated, may hold values from 0.25 to 1.75
- expert_ids: int32 [256, 1], P('expert'), may hold values from 0 to 15; in each aligned block of 16 rows (0 to 15, 16 to 31, ...) at most 2 rows name the same one
- w_in: bfloat16 [16, 4096, 2048], P('expert', None, 'mp'), may hold values from -0.09375 to 0.09375
- w_out: bfloat16 [16, 2048, 4096], P('expert', 'mp'), may hold values from -0.125 to 0.125
- queries: bfloat16 [256, 2048], P('expert', 'mp'), may hold values from -4.5 to 4.5
- keys: bfloat16 [256, 128, 512], P('expert', None, 'mp'), may hold values from -4.5 to 4.5
- values: bfloat16 [256, 128, 512], P('expert', None, 'mp'), may hold values from -6 to 6
- new_keys: bfloat16 [256, 512], P('expert', 'mp'), may hold values from -9 to 9
- new_values: bfloat16 [256, 512], P('expert', 'mp'), may hold values from -6 to 6
- cache_lengths: int32 [256], P('expert'), may hold values from 32 to 128, as said below
Outputs:
- mixed: bfloat16 [256, 4096], P('expert', 'mp')
- attended: bfloat16 [256, 2048], P('expert', 'mp')
Inputs may be any that keep to these rules, and one draw needn't show every extreme that they name: `expert_ids`: in each aligned block of 16 tokens (the tokens of one index of expert) no expert is named more than 2 times, a bound that some block reaches. `cache_lengths`: some sequence has all 128 positions filled.
All inputs are finite; a program needn't handle non-finite values.
Results may differ from a plain program's by a relative error of at most 0.0055.
Values may be sent and summed in bfloat16 or wider, within the bound.
A program may use at most 128 MiB of HBM per device.

v0:
```python
import jax
import jax.numpy as jnp
from jax import lax
from jax.sharding import PartitionSpec as P

HEAD = 128
CAP = 2


def attend_local(queries, keys, values, new_keys, new_values, cache_lengths):
    seq_count = queries.shape[0]
    ctx_len = keys.shape[1]
    kv_local = keys.shape[2] // HEAD
    group_size = queries.shape[1] // (kv_local * HEAD)
    score_scale = HEAD ** (-0.5)
    query_heads = queries.reshape(seq_count, kv_local, group_size, HEAD)
    key_heads = keys.reshape(seq_count, ctx_len, kv_local, HEAD)
    value_heads = values.reshape(seq_count, ctx_len, kv_local, HEAD)
    newkey_heads = new_keys.reshape(seq_count, kv_local, HEAD)
    newvalue_heads = new_values.reshape(seq_count, kv_local, 1, HEAD).astype(jnp.float32)
    scores = (
        jnp.einsum("skgd,sckd->skgc", query_heads, key_heads, preferred_element_type=jnp.float32)
        * score_scale
    )
    own_score = (
        jnp.einsum("skgd,skd->skg", query_heads, newkey_heads, preferred_element_type=jnp.float32)
        * score_scale
    )
    visible = (jnp.arange(ctx_len, dtype=jnp.int32)[None, :] < cache_lengths[:, None])[
        :, None, None, :
    ]
    scores = jnp.where(visible, scores, -1e30)
    highest = jnp.maximum(jnp.max(scores, axis=-1), own_score)
    cache_terms = jnp.exp(scores - highest[..., None])
    own_term = jnp.exp(own_score - highest)
    denominator = jnp.sum(cache_terms, axis=-1) + own_term
    weights = (cache_terms / denominator[..., None]).astype(jnp.bfloat16)
    own_weight = (own_term / denominator).astype(jnp.bfloat16)
    output = jnp.einsum("skgc,sckd->skgd", weights, value_heads, preferred_element_type=jnp.float32)
    output = output + own_weight.astype(jnp.float32)[..., None] * newvalue_heads
    return output.reshape(seq_count, queries.shape[1]).astype(jnp.bfloat16)


def shards(
    tokens,
    norm_gain,
    expert_ids,
    w_in,
    w_out,
    queries,
    keys,
    values,
    new_keys,
    new_values,
    cache_lengths,
):
    model_width = tokens.shape[1]
    residual = tokens.astype(jnp.float32)
    mean_square = jnp.mean(residual * residual, axis=-1, keepdims=True)
    normed = (
        residual * lax.rsqrt(mean_square + 1e-05) * norm_gain.astype(jnp.float32)[None, :]
    ).astype(jnp.bfloat16)
    expert_count = lax.axis_size("expert") * w_in.shape[0]
    expert_row = expert_ids[:, 0]
    onehot = (expert_row[:, None] == jnp.arange(expert_count, dtype=jnp.int32)[None, :]).astype(
        jnp.int32
    )
    earlier = jnp.cumsum(onehot, axis=0) - onehot
    slot_index = jnp.sum(earlier * onehot, axis=1)
    target = expert_row * CAP + slot_index
    placed = (target[None, :] == jnp.arange(expert_count * CAP, dtype=jnp.int32)[:, None]).astype(
        jnp.bfloat16
    )
    outgoing = jnp.dot(placed, normed, preferred_element_type=jnp.float32).astype(jnp.bfloat16)
    outgoing = outgoing.reshape(expert_count, CAP, model_width)
    half_width = model_width // lax.axis_size("mp")
    offset = lax.axis_index("mp") * half_width
    arrived = lax.all_to_all(outgoing, "expert", split_axis=0, concat_axis=0, tiled=True)
    sources = arrived.shape[0]
    slot_count = arrived.shape[1]
    flat_rows = arrived.reshape(sources * slot_count, model_width)
    hidden = jnp.maximum(
        jnp.dot(flat_rows, w_in[0], preferred_element_type=jnp.float32), 0.0
    ).astype(jnp.bfloat16)
    partial_value = jnp.dot(hidden, w_out[0], preferred_element_type=jnp.float32).reshape(
        sources, slot_count, model_width
    )
    summed = lax.psum_scatter(partial_value, "mp", scatter_dimension=2, tiled=True)
    returned = lax.all_to_all(
        summed.astype(jnp.bfloat16), "expert", split_axis=0, concat_axis=0, tiled=True
    )
    contract_rows = (((0,), (0,)), ((), ()))
    back_rows = returned.reshape(expert_count * CAP, half_width)
    expert_out = lax.dot_general(
        placed, back_rows, contract_rows, preferred_element_type=jnp.float32
    )
    residual_half = lax.dynamic_slice_in_dim(residual, offset, half_width, 1)
    mixed = (residual_half + expert_out).astype(jnp.bfloat16)
    attended = attend_local(queries, keys, values, new_keys, new_values, cache_lengths)
    return (mixed, attended)


def solution(mesh):
    return jax.shard_map(
        shards,
        mesh=mesh,
        in_specs=(
            P("expert", None),
            P(),
            P("expert", None),
            P("expert", None, "mp"),
            P("expert", "mp", None),
            P("expert", "mp"),
            P("expert", None, "mp"),
            P("expert", None, "mp"),
            P("expert", "mp"),
            P("expert", "mp"),
            P("expert"),
        ),
        out_specs=(P("expert", "mp"), P("expert", "mp")),
        check_vma=False,
    )
```

profile of v0, /device:TPU:0, one launch (start us, length us, event | category | flops | bytes accessed | tf_op | source)
XLA Modules:
  0.0 72.7 jit_solution(16995123466417724180)
XLA Ops:
  7.2 0.0 copy-start
  7.2 0.8 %convert_element_type.53 = f32[4096]{0:T(1024)S(1)} convert(bf16[4096]{0:T(1024)(128)(2,1)} %param.12) | non-fusion elementwise | flops 4096 | bytes 24576 | tf_op jit(solution)/shard_map/convert_element_type | solution.py:61
  8.0 1.0 %multiply_reduce_fusion = f32[16]{0:T(128)S(1)} fusion(bf16[16,4096]{1,0:T(8,128)(2,1)} %param.11), kind=kLoop, calls=%fused_computation.18 | loop fusion | flops 196592 | bytes 131136 | tf_op jit(solution)/shard_map/reduce_sum | solution.py:59
  9.0 0.7 %fusion.26 = s32[16,16]{1,0:T(8,128)S(1)} fusion(s32[16]{0:T(128)} %bitcast.38), kind=kLoop, calls=%fused_computation.37 | loop fusion | flops 512 | bytes 1088 | tf_op jit(solution)/shard_map/convert_element_type | solution.py:65
  9.8 0.8 %select_reduce_fusion = s32[16]{0:T(128)S(1)} fusion(s32[16,16]{1,0:T(8,128)S(1)} %reduce_window_sum.11, s32[16]{0:T(128)} %bitcast.39), kind=kLoop, calls=%fused_computation.35 | loop fusion | flops 1264 | bytes 1152 | tf_op jit(solution)/shard_map/reduce_sum | solution.py:69
  10.6 0.7 multiply_add_fusion
  11.3 1.2 %convolution_convert_fusion = bf16[32,4096]{1,0:T(8,128)(2,1)S(1)} fusion(f32[4096]{0:T(1024)S(1)} %convert_element_type.53, f32[16]{0:T(128)S(1)} %add_rsqrt_fusion, bf16[16,4096]{1,0:T(8,128)(2,1)} %param.11, s32[16]{0:T(128)S(1)} %multiply_add_fusion), kind=kOutput, calls=%fused_computation.4 | convolution fusion | flops 4588032 | bytes 409728 | tf_op jit(solution)/shard_map/dot_general | solution.py:74
  12.5 0.9 %reshape.76 = bf16[16,2,4096]{2,1,0:T(2,128)(2,1)} reshape(bf16[32,4096]{1,0:T(8,128)(2,1)S(1)} %convolution_convert_fusion) | data formatting | bytes 524288 | tf_op jit(solution)/shard_map/reshape | solution.py:75
  13.4 8.3 %all-to-all-start = ((bf16[16,2,4096]{2,1,0:T(2,128)(2,1)}), bf16[16,2,4096]{2,1,0:T(2,128)(2,1)S(1)}, u32[]{:S(2)}, u32[]{:S(2)}) async-start(bf16[16,2,4096]{2,1,0:T(2,128)(2,1)} %reshape.76), calls=%async_computation | async-start | bytes 524288 | tf_op jit(solution)/shard_map/all_to_all | solution.py:78
  21.7 0.0 reduce-scatter.2.cloned.1.call-start
  21.8 0.9 %convert_element_type.51 = f32[16,4096]{1,0:T(8,128)S(1)} convert(bf16[16,4096]{1,0:T(8,128)(2,1)} %param.11) | non-fusion elementwise | flops 65536 | bytes 393216 | tf_op jit(solution)/shard_map/convert_element_type | solution.py:58
  22.7 0.8 %reshape.79 = bf16[16,2,4,128]{3,2,1,0:T(4,128)(2,1)S(1)} reshape(bf16[16,1024]{1,0:T(8,128)(2,1)} %param.16) | data formatting | bytes 65536 | tf_op jit(solution)/shard_map/reshape | solution.py:16
  23.5 0.7 reshape.83
  24.2 0.7 reshape.88
  24.9 0.1 fusion.30
  25.0 6.5 %all-to-all-done = bf16[16,2,4096]{2,1,0:T(2,128)(2,1)S(1)} async-done(((bf16[16,2,4096]{2,1,0:T(2,128)(2,1)}), bf16[16,2,4096]{2,1,0:T(2,128)(2,1)S(1)}, u32[]{:S(2)}, u32[]{:S(2)}) %all-to-all-start) | async-done | bytes 262176 | tf_op jit(solution)/shard_map/all_to_all | solution.py:78
  31.6 0.1 reshape.77
  31.7 4.9 %fusion.8 = bf16[32,1024]{1,0:T(8,128)(2,1)S(1)} fusion(bf16[32,4096]{1,0:T(8,128)(2,1)S(1)} %reshape.77, bf16[1,4096,1024]{2,1,0:T(8,128)(2,1)} %param.14), kind=kOutput, calls=%fused_computation.8 | convolution fusion | flops 268500992 | bytes 8716288 | tf_op jit(solution)/shard_map/dot_general | solution.py:83
  36.7 5.8 %fusion = f32[16,2,4096]{2,0,1:T(8,128)} fusion(bf16[1,1024,4096]{2,1,0:T(8,128)(2,1)} %param.15, bf16[16,2,1024]{2,1,0:T(2,128)(2,1)S(1)} %dot_general.25), kind=kOutput, calls=%fused_computation | convolution fusion | flops 268435456 | bytes 8978432 | tf_op jit(solution)/shard_map/dot_general | solution.py:85
  42.5 0.0 reduce-scatter.2.cloned.1.call-update
  42.5 0.1 iota_compare_fusion.3
  42.6 0.7 %fusion.29 = (f32[16,2,4]{2,1,0:T(2,128)S(1)}, f32[16,2,4,128]{3,2,1,0:T(4,128)S(1)}) fusion(bf16[16,2,4,128]{3,2,1,0:T(4,128)(2,1)S(1)} %reshape.79, pred[16,128]{1,0:T(8,128)(4,1)S(1)} %iota_compare_fusion.3, bf16[16,128,256]{2,1,0:T(8,128)(2,1)S(1)} %copy-done), kind=kOutput, calls=%fused_computation.42 | convolution fusion | flops 4243328 | bytes 1149440 | tf_op jit(solution)/shard_map/skgd,sckd->skgc/dot_general | solution.py:22
  43.4 0.2 fusion.21
  43.6 4.9 %reduce-scatter.2.cloned.1.call-done = f32[16,2,2048]{2,0,1:T(8,128)} async-done(((f32[16,2,4096]{2,0,1:T(8,128)}), f32[16,2,2048]{2,0,1:T(8,128)}) %reduce-scatter.2.cloned.1.call-update) | async-done | bytes 262160 | tf_op jit(solution)/shard_map/reduce_scatter | solution.py:88
  48.5 1.0 %convert_element_type.57 = bf16[16,2,2048]{2,0,1:T(8,128)(2,1)S(1)} convert(f32[16,2,2048]{2,0,1:T(8,128)} %reduce-scatter.2.cloned.1.call-done) | non-fusion elementwise | flops 65536 | bytes 393216 | tf_op jit(solution)/shard_map/convert_element_type | solution.py:90
  49.5 0.8 %copy.21 = bf16[16,2,2048]{2,1,0:T(2,128)(2,1)} copy(bf16[16,2,2048]{2,0,1:T(8,128)(2,1)S(1)} %convert_element_type.57) | data formatting | bytes 262144 | tf_op jit(solution)/shard_map/convert_element_type | solution.py:90
  50.3 6.7 %all-to-all-start.1 = ((bf16[16,2,2048]{2,1,0:T(2,128)(2,1)}), bf16[16,2,2048]{2,1,0:T(2,128)(2,1)S(1)}, u32[]{:S(2)}, u32[]{:S(2)}) async-start(bf16[16,2,2048]{2,1,0:T(2,128)(2,1)} %copy.21), calls=%async_computation.2 | async-start | bytes 262144 | tf_op jit(solution)/shard_map/all_to_all | solution.py:89
  57.0 0.4 fusion.12
  57.5 0.6 convert_element_type.65
  58.1 6.9 %all-to-all-done.1 = bf16[16,2,2048]{2,1,0:T(2,128)(2,1)S(1)} async-done(((bf16[16,2,2048]{2,1,0:T(2,128)(2,1)}), bf16[16,2,2048]{2,1,0:T(2,128)(2,1)S(1)}, u32[]{:S(2)}, u32[]{:S(2)}) %all-to-all-start.1) | async-done | bytes 131104 | tf_op jit(solution)/shard_map/all_to_all | solution.py:89
  65.0 0.1 reshape.78
  65.0 0.9 %fusion.4 = bf16[16,2048]{1,0:T(8,128)(2,1)} fusion(bf16[32,2048]{1,0:T(8,128)(2,1)S(1)} %reshape.78, f32[16,4096]{1,0:T(8,128)S(1)} %convert_element_type.51, s32[]{:T(128)S(6)} %select_n.7, s32[16]{0:T(128)S(1)} %multiply_add_fusion), kind=kOutput, calls=%fused_computation.6 | convolution fusion | flops 2163200 | bytes 327748 | tf_op jit(solution)/shard_map/dot_general | solution.py:94
  (10 shorter events, 0.1 us)
Async XLA Ops:
  7.2 35.4 %copy-start = (bf16[16,128,256]{2,1,0:T(8,128)(2,1)S(1)}, bf16[16,128,256]{2,1,0:T(8,128)(2,1)}, u32[]{:S(2)}) copy-start(bf16[16,128,256]{2,1,0:T(8,128)(2,1)} %param.17) | copy-start | bytes 3145732
  13.4 18.2 %all-to-all-start = ((bf16[16,2,4096]{2,1,0:T(2,128)(2,1)}), bf16[16,2,4096]{2,1,0:T(2,128)(2,1)S(1)}, u32[]{:S(2)}, u32[]{:S(2)}) async-start(bf16[16,2,4096]{2,1,0:T(2,128)(2,1)} %reshape.76), calls=%async_computation | async-start | bytes 524288 | tf_op jit(solution)/shard_map/all_to_all | solution.py:78
  21.7 26.8 %reduce-scatter.2.cloned.1.call-start = ((), (), s32[]{:S(2)}) async-start(), calls=%async_computation.3 | async-start | bytes 786432 | tf_op jit(solution)/shard_map/reduce_scatter | solution.py:88
  36.6 5.9 %copy-start.1 = (s32[16]{0:T(128)S(1)}, s32[16]{0:T(128)}, u32[]{:S(2)}) copy-start(s32[16]{0:T(128)} %param.21) | copy-start | bytes 196
  36.6 20.4 %copy-start.2 = (bf16[16,128,256]{2,1,0:T(8,128)(2,1)S(1)}, bf16[16,128,256]{2,1,0:T(8,128)(2,1)}, u32[]{:S(2)}) copy-start(bf16[16,128,256]{2,1,0:T(8,128)(2,1)} %param.18) | copy-start | bytes 3145732
  50.3 14.7 %all-to-all-start.1 = ((bf16[16,2,2048]{2,1,0:T(2,128)(2,1)}), bf16[16,2,2048]{2,1,0:T(2,128)(2,1)S(1)}, u32[]{:S(2)}, u32[]{:S(2)}) async-start(bf16[16,2,2048]{2,1,0:T(2,128)(2,1)} %copy.21), calls=%async_computation.2 | async-start | bytes 262144 | tf_op jit(solution)/shard_map/all_to_all | solution.py:89
Sparse Core Ops, SparseCore 0:
  42.6 5.8 reduce-scatter.1
where the time goes:
time: 73.3 us; the launch traced here: 72.7 us
  waiting for transfers between devices  18.3 us (25%)
  starting transfers between devices  15.1 us (21%)
  matrix products  14.1 us (19%)
  between operations  14.1 us (19%)
  other arithmetic  6.35 us (9%)
  local copies, waits for them, and re-layouts  4.7 us (6%)
    all_to_all x1, starting transfers between devices, shards(): lax.all_to_all(outgoing, 'expert', split_axis=0, concat_axis=0, tiled=True)  8.34 us
    all_to_all x1, waiting for transfers between devices, shards(): lax.all_to_all(summed.astype(jnp.bfloat16), 'expert', split_axis=0, conca...  6.86 us
    all_to_all x1, starting transfers between devices, shards(): lax.all_to_all(summed.astype(jnp.bfloat16), 'expert', split_axis=0, conca...  6.73 us
    all_to_all x1, waiting for transfers between devices, shards(): lax.all_to_all(outgoing, 'expert', split_axis=0, concat_axis=0, tiled=True)  6.54 us
    dot_general x1, matrix products, shards(): jnp.dot(hidden, w_out[0], preferred_element_type=jnp.float32)  5.8 us
    dot_general x1, matrix products, shards(): jnp.dot(flat_rows, w_in[0], preferred_element_type=jnp.float32)  4.93 us
    reduce_scatter x1, waiting for transfers between devices, shards(): lax.psum_scatter(partial_value, 'mp', scatter_dimension=2, tiled=True)  4.89 us
  transfers between devices with their start and end apart: 3, of which 3 were waited for; matrix products, arithmetic and copies ran while one was open for 7% of the time, Pallas kernels for 0%

commit v1 on v0

v1 whole, which is shorter than its diff:
```python
import functools

import jax
import jax.numpy as jnp
from jax import lax
from jax.experimental import pallas as pl
from jax.experimental.pallas import tpu as pltpu
from jax.sharding import PartitionSpec as P

HEAD = 128
CAP = 2
RETURN_PIECES = 2
F32 = jnp.float32
BF16 = jnp.bfloat16
MESH = pl.DeviceIdType.MESH


def step_kernel(
    experts,
    lens,
    tok_h,
    gain_h,
    ids_h,
    win_h,
    wout_h,
    q_h,
    k_h,
    v_h,
    nk_h,
    nv_h,
    mixed,
    att,
    tok,
    gain,
    ids,
    win,
    wout,
    q,
    k,
    v,
    nk,
    nv,
    out2d,
    outgoing,
    arrived,
    relayed,
    x_own,
    x_other,
    hidden_part,
    part_send,
    part_recv,
    ret2d,
    ret,
    back,
    back2d,
    q_rows,
    nk_rows,
    nv_rows,
    score_rows,
    own_rows,
    att_rows,
    load_sem,
    send_sem,
    recv_sem,
    relay_send,
    relay_recv,
    part_ssem,
    part_rsem,
    ret_send,
    ret_recv,
):
    rows, width = tok.shape
    half = width // 2
    me = lax.axis_index("expert")
    core = lax.axis_index("mp")
    other = 1 - core
    own_off = pl.multiple_of(core * half, half)
    other_off = pl.multiple_of(other * half, half)
    slots = experts * CAP

    loads = [
        pltpu.make_async_copy(src, dst, load_sem.at[n])
        for n, (src, dst) in enumerate(
            [
                (tok_h, tok),
                (ids_h, ids),
                (gain_h, gain),
                (q_h, q),
                (nk_h, nk),
                (nv_h, nv),
                (k_h, k),
                (v_h, v),
                (win_h.at[0, pl.ds(own_off, half), :], win.at[0]),
                (win_h.at[0, pl.ds(other_off, half), :], win.at[1]),
                (wout_h.at[0, :, pl.ds(other_off, half)], wout.at[0]),
                (wout_h.at[0, :, pl.ds(own_off, half)], wout.at[1]),
            ]
        )
    ]
    for load in loads[:3]:
        load.start()

    barrier = pltpu.get_barrier_semaphore()
    for i in range(1, experts):
        pl.semaphore_signal(
            barrier, inc=1, device_id=(lax.rem(me + i, experts), core), device_id_type=MESH
        )
    pl.semaphore_signal(barrier, inc=1, device_id=(me, other), device_id_type=MESH)
    for load in loads[3:]:
        load.start()

    for load in loads[:3]:
        load.wait()
    whole = tok[...].astype(F32)
    inverse = lax.rsqrt(jnp.mean(whole * whole, axis=-1, keepdims=True) + 1e-05)
    mine = tok[:, pl.ds(own_off, half)].astype(F32)
    normed = (mine * inverse * gain[:, pl.ds(own_off, half)].astype(F32)).astype(BF16)
    relative = ids[...] - me
    relative = jnp.where(relative < 0, relative + experts, relative)
    onehot = relative == lax.broadcasted_iota(jnp.int32, (rows, experts), 1)
    onehot = jnp.where(onehot, 1.0, 0.0)
    r_i = lax.broadcasted_iota(jnp.int32, (rows, rows), 0)
    c_i = lax.broadcasted_iota(jnp.int32, (rows, rows), 1)
    below = jnp.where(c_i < r_i, 1.0, 0.0).astype(BF16)
    earlier = jnp.dot(below, onehot.astype(BF16), preferred_element_type=F32)
    slot = jnp.sum(earlier * onehot, axis=1, keepdims=True)
    target = relative.astype(F32) * CAP + slot
    placed_t = jnp.where(
        target == lax.broadcasted_iota(jnp.int32, (rows, slots), 1).astype(F32), 1.0, 0.0
    ).astype(BF16)
    spread = jnp.where(r_i == c_i, target, 0.0).astype(BF16)
    target_rows = jnp.dot(jnp.ones((slots, rows), BF16), spread, preferred_element_type=F32)
    placed = jnp.where(
        target_rows == lax.broadcasted_iota(jnp.int32, (slots, rows), 0).astype(F32), 1.0, 0.0
    ).astype(BF16)
    out2d[...] = jnp.dot(placed, normed, preferred_element_type=F32).astype(BF16)
    for i in range(experts):
        outgoing[i] = out2d[CAP * i : CAP * (i + 1), :]

    pl.semaphore_wait(barrier, experts)

    def relay(i):
        return pltpu.make_async_remote_copy(
            src_ref=outgoing.at[0] if i == 0 else arrived.at[i],
            dst_ref=relayed.at[i],
            send_sem=relay_send.at[i],
            recv_sem=relay_recv.at[i],
            device_id=(me, other),
            device_id_type=MESH,
        )

    def send(i):
        return pltpu.make_async_remote_copy(
            src_ref=outgoing.at[i],
            dst_ref=arrived.at[i],
            send_sem=send_sem.at[i],
            recv_sem=recv_sem.at[i],
            device_id=(lax.rem(me + i, experts), core),
            device_id_type=MESH,
        )

    for i in range(1, experts):
        send(i).start()
    relay(0).start()
    x_own[0:CAP, :] = out2d[0:CAP, :]

    kv_heads = nk.shape[1] // HEAD
    heads = q.shape[1] // HEAD
    group = heads // kv_heads
    ctx = k.shape[1]
    for load in loads[3:7]:
        load.wait()
    for h in range(heads):
        q_rows[h * rows : (h + 1) * rows, :] = q[:, h * HEAD : (h + 1) * HEAD].astype(F32)
    nk_rows[...] = nk[...].astype(F32)
    nv_rows[...] = nv[...].astype(F32)
    lane = lax.broadcasted_iota(jnp.int32, (heads, ctx), 1)
    head_of = lax.broadcasted_iota(jnp.int32, (heads, HEAD), 0) // group
    scale = HEAD ** (-0.5)

    def attend_scores(lo, hi):
        for s in range(lo, hi):
            q_s = q_rows[pl.ds(s, heads, stride=rows), :]
            wide = jnp.concatenate(
                [jnp.where(head_of == j, q_s, 0.0) for j in range(kv_heads)], axis=1
            )
            scores = lax.dot_general(
                wide.astype(BF16), k[s], (((1,), (1,)), ((), ())), preferred_element_type=F32
            )
            own = jnp.sum(wide * nk_rows[s : s + 1, :], axis=1, keepdims=True)
            score_rows[s * heads : (s + 1) * heads, :] = jnp.where(
                lane < lens[s], scores * scale, -1e30
            )
            own_rows[s * heads : (s + 1) * heads, :] = own * scale

    def attend_values(lo, hi):
        part = slice(lo * heads, hi * heads)
        scores = score_rows[part, :]
        own = own_rows[part, :]
        highest = jnp.maximum(jnp.max(scores, axis=1, keepdims=True), own)
        terms = jnp.exp(scores - highest)
        own_term = jnp.exp(own - highest)
        total = jnp.sum(terms, axis=1, keepdims=True) + own_term
        weights = (terms / total).astype(BF16)
        own_weight = (own_term / total).astype(BF16).astype(F32)
        for s in range(lo, hi):
            at = (s - lo) * heads
            full = jnp.dot(weights[at : at + heads, :], v[s], preferred_element_type=F32)
            full = full + own_weight[at : at + heads, :] * nv_rows[s : s + 1, :]
            picked = full[:, 0:HEAD]
            for j in range(1, kv_heads):
                picked = jnp.where(head_of == j, full[:, j * HEAD : (j + 1) * HEAD], picked)
            att_rows[pl.ds(s, heads, stride=rows), :] = picked

    attend_scores(0, rows)

    for i in range(1, experts):
        send(i).wait_recv()
        relay(i).start()
        x_own[CAP * i : CAP * (i + 1), :] = arrived[i]
    loads[8].wait()
    hidden_part[...] = jnp.dot(x_own[...], win[0], preferred_element_type=F32)
    for i in range(experts):
        relay(i).wait_recv()
        x_other[CAP * i : CAP * (i + 1), :] = relayed[i]
    loads[9].wait()
    hidden = jnp.maximum(
        hidden_part[...] + jnp.dot(x_other[...], win[1], preferred_element_type=F32), 0.0
    ).astype(BF16)

    piece = half // RETURN_PIECES

    def part_copy(c):
        return pltpu.make_async_remote_copy(
            src_ref=part_send.at[c],
            dst_ref=part_recv.at[c],
            send_sem=part_ssem.at[c],
            recv_sem=part_rsem.at[c],
            device_id=(me, other),
            device_id_type=MESH,
        )

    def give_back(c, i):
        return pltpu.make_async_remote_copy(
            src_ref=ret.at[c, i],
            dst_ref=back.at[c, i],
            send_sem=ret_send.at[c, i],
            recv_sem=ret_recv.at[c, i],
            device_id=(lax.rem(me + experts - i, experts), core),
            device_id_type=MESH,
        )

    loads[10].wait()
    for c in range(RETURN_PIECES):
        part_send[c] = jnp.dot(
            hidden, wout[0, :, c * piece : (c + 1) * piece], preferred_element_type=F32
        ).astype(BF16)
        part_copy(c).start()
    loads[11].wait()
    for c in range(RETURN_PIECES):
        cols = slice(c * piece, (c + 1) * piece)
        own_part = jnp.dot(hidden, wout[1, :, cols], preferred_element_type=F32)
        part_copy(c).wait_recv()
        ret2d[c] = (own_part + part_recv[c].astype(F32)).astype(BF16)
        for i in range(1, experts):
            ret[c, i] = ret2d[c, CAP * i : CAP * (i + 1), :]
            give_back(c, i).start()
        back2d[0:CAP, cols] = ret2d[c, 0:CAP, :]

    loads[7].wait()
    attend_values(0, rows)
    for h in range(heads):
        att[:, h * HEAD : (h + 1) * HEAD] = att_rows[h * rows : (h + 1) * rows, :].astype(BF16)

    for c in range(RETURN_PIECES):
        cols = slice(c * piece, (c + 1) * piece)
        for i in range(1, experts):
            give_back(c, i).wait_recv()
            back2d[CAP * i : CAP * (i + 1), cols] = back[c, i]
        expert_out = jnp.dot(placed_t, back2d[:, cols], preferred_element_type=F32)
        at = pl.multiple_of(own_off + c * piece, piece)
        mixed[:, cols] = (tok[:, pl.ds(at, piece)].astype(F32) + expert_out).astype(BF16)

    for i in range(1, experts):
        send(i).wait_send()
    for i in range(experts):
        relay(i).wait_send()
    for c in range(RETURN_PIECES):
        part_copy(c).wait_send()
        for i in range(1, experts):
            give_back(c, i).wait_send()


def shards(tokens, norm_gain, expert_ids, w_in, w_out, queries, keys, values, new_keys, new_values, lens):
    experts = lax.axis_size("expert")
    rows, width = tokens.shape
    half = width // 2
    inner = w_in.shape[2]
    slots = experts * CAP
    heads = queries.shape[1] // HEAD
    ctx = keys.shape[1]
    piece = half // RETURN_PIECES
    dma = pltpu.SemaphoreType.DMA
    gain = norm_gain.reshape(1, width)
    any_spec = pl.BlockSpec(memory_space=pl.ANY)
    vmem = pl.BlockSpec(memory_space=pltpu.VMEM)
    like = lambda a: pltpu.VMEM(a.shape, a.dtype)
    return pl.pallas_call(
        functools.partial(step_kernel, experts),
        out_shape=(
            jax.ShapeDtypeStruct((rows, half), BF16),
            jax.ShapeDtypeStruct(queries.shape, BF16),
        ),
        in_specs=[pl.BlockSpec(memory_space=pltpu.SMEM)] + [any_spec] * 10,
        out_specs=(vmem, vmem),
        scratch_shapes=[
            like(tokens),
            like(gain),
            like(expert_ids),
            pltpu.VMEM((2, half, inner), BF16),
            pltpu.VMEM((2, inner, half), BF16),
            like(queries),
            like(keys),
            like(values),
            like(new_keys),
            like(new_values),
            pltpu.VMEM((slots, half), BF16),
            pltpu.VMEM((experts, CAP, half), BF16),
            pltpu.VMEM((experts, CAP, half), BF16),
            pltpu.VMEM((experts, CAP, half), BF16),
            pltpu.VMEM((slots, half), BF16),
            pltpu.VMEM((slots, half), BF16),
            pltpu.VMEM((slots, inner), F32),
            pltpu.VMEM((RETURN_PIECES, slots, piece), BF16),
            pltpu.VMEM((RETURN_PIECES, slots, piece), BF16),
            pltpu.VMEM((RETURN_PIECES, slots, piece), BF16),
            pltpu.VMEM((RETURN_PIECES, experts, CAP, piece), BF16),
            pltpu.VMEM((RETURN_PIECES, experts, CAP, piece), BF16),
            pltpu.VMEM((slots, half), BF16),
            pltpu.VMEM((heads * rows, HEAD), F32),
            pltpu.VMEM(new_keys.shape, F32),
            pltpu.VMEM(new_values.shape, F32),
            pltpu.VMEM((heads * rows, ctx), F32),
            pltpu.VMEM((heads * rows, 1), F32),
            pltpu.VMEM((heads * rows, HEAD), F32),
            dma((12,)),
            dma((experts,)),
            dma((experts,)),
            dma((experts,)),
            dma((experts,)),
            dma((RETURN_PIECES,)),
            dma((RETURN_PIECES,)),
            dma((RETURN_PIECES, experts)),
            dma((RETURN_PIECES, experts)),
        ],
        compiler_params=pltpu.CompilerParams(
            collective_id=0, has_side_effects=True, vmem_limit_bytes=60 * 1024 * 1024
        ),
    )(lens, tokens, gain, expert_ids, w_in, w_out, queries, keys, values, new_keys, new_values)


def solution(mesh):
    return jax.shard_map(
        shards,
        mesh=mesh,
        in_specs=(
            P("expert", None),
            P(),
            P("expert", None),
            P("expert", None, "mp"),
            P("expert", "mp", None),
            P("expert", "mp"),
            P("expert", None, "mp"),
            P("expert", None, "mp"),
            P("expert", "mp"),
            P("expert", "mp"),
            P("expert"),
        ),
        out_specs=(P("expert", "mp"), P("expert", "mp")),
        check_vma=False,
    )
```

time: 73.3 us -> 31.5 us (0.43)
  Pallas kernels: 0 us -> 25.1 us
  waiting for transfers between devices: 18.3 us -> 0 us
  starting transfers between devices: 15.1 us -> 0 us
  matrix products: 14.1 us -> 0 us
  between operations: 14.1 us -> 0.64 us
  other arithmetic: 6.35 us -> 0 us
  local copies, waits for them, and re-layouts: 4.7 us -> 5.49 us
    pallas_call x0 -> x1, Pallas kernels: none -> 25.1 us  [shards(): pl.pallas_call(functools.partial(step_kernel, experts), out_shape=(jax.Sh...]
    all_to_all x2 -> x0, starting transfers between devices: 15.1 us -> none  [the longest x1 8.34 us: shards(): lax.all_to_all(outgoing, 'expert', split_axis=0, concat_axis=0, tiled=True)]
    dot_general x7 -> x0, matrix products: 14.1 us -> none  [the longest x1 5.8 us: shards(): jnp.dot(hidden, w_out[0], preferred_element_type=jnp.float32)]
    all_to_all x2 -> x0, waiting for transfers between devices: 13.4 us -> none  [the longest x1 6.86 us: shards(): lax.all_to_all(summed.astype(jnp.bfloat16), 'expert', split_axis=0, conca...]
    reduce_scatter x1 -> x0, waiting for transfers between devices: 4.89 us -> none  [shards(): lax.psum_scatter(partial_value, 'mp', scatter_dimension=2, tiled=True)]
    unnamed x6 -> x3, local copies, waits for them, and re-layouts: 0.02 us -> 4.18 us
    convert_element_type x4 -> x0, other arithmetic: 3.41 us -> none  [the longest x1 0.96 us: shards(): summed.astype(jnp.bfloat16)]
    convert_element_type x3 -> x0, local copies, waits for them, and re-layouts: 2.13 us -> none  [the longest x1 0.77 us: shards(): summed.astype(jnp.bfloat16)]
  transfers between devices with their start and end apart: 3 -> 0, of which waited for: 3 -> 0; matrix products, arithmetic and copies ran while one was open for 7% -> 0% of each run, Pallas kernels for 0% -> 0%
where the time goes in v1:
time: 31.5 us; the launch traced here: 31.2 us
  Pallas kernels  25.1 us (80%)
  local copies, waits for them, and re-layouts  5.49 us (17%)
  between operations  0.64 us (2%)
    pallas_call x1, Pallas kernels, shards(): pl.pallas_call(functools.partial(step_kernel, experts), out_shape=(jax.Sh...  25.1 us
    unnamed x3, local copies, waits for them, and re-layouts  4.18 us
    reshape x1, local copies, waits for them, and re-layouts, shards(): gain = norm_gain.reshape(1, width)  1.31 us

profile of v1, /device:TPU:0, one launch (start us, length us, event | category | flops | bytes accessed | tf_op | source)
XLA Modules:
  0.0 31.2 jit_solution(9408916483819534836)
XLA Ops:
  0.6 1.3 %copy.13.ids_h = s32[16,1]{1,0:T(8,128)} copy(s32[16,1]{0,1:T(1,128)} %param.13) | data formatting | bytes 128 | tf_op args[2]
  2.0 1.3 %reshape.7.gain_h = bf16[1,4096]{1,0:T(2,128)(2,1)} reshape(bf16[4096]{0:T(1024)(128)(2,1)} %param.12) | data formatting | bytes 16384 | tf_op jit(solution)/shard_map/reshape | solution.py:304
  3.3 25.1 %shard_map.122 = (bf16[16,2048]{1,0:T(8,128)(2,1)}, bf16[16,1024]{1,0:T(8,128)(2,1)}) custom-call(s32[16]{0:T(128)} %lens.1, bf16[16,4096]{1,0:T(8,128)(2,1)} %tok_h.1, bf16[1,4096]{1,0:T(2,128)(2,1)} %reshape.7.gain_h, s32[16,1]{1,0:T(8,128)} %copy.13.ids_h, bf16[1,4096,1024]{2,1,0:T(8,128)(2,1)} %win_h.1, bf16[1,1024,4096]{2,1,0:T(8,128)(2,1)} %wout_h.1, ...), custom_call_target="tpu_custom_call" | custom-call | tf_op jit(solution)/shard_map/pallas_call | solution.py:308
  28.4 1.5 %copy.16 = bf16[16,2048]{1,0:T(8,128)(2,1)} copy(bf16[16,2048]{1,0:T(8,128)(2,1)} %get-tuple-element.4) | data formatting | bytes 131072
  29.8 1.4 %copy.17 = bf16[16,1024]{1,0:T(8,128)(2,1)} copy(bf16[16,1024]{1,0:T(8,128)(2,1)} %get-tuple-element.5) | data formatting | bytes 65536

commit v2 on v1

--- a/solution.py
+++ b/solution.py
@@ -114,24 +114,24 @@
     whole = tok[...].astype(F32)
     inverse = lax.rsqrt(jnp.mean(whole * whole, axis=-1, keepdims=True) + 1e-05)
     mine = tok[:, pl.ds(own_off, half)].astype(F32)
-    normed = (mine * inverse * gain[:, pl.ds(own_off, half)].astype(F32)).astype(BF16)
+    normed = (mine * inverse * gain[pl.ds(own_off, half)].astype(F32)[None, :]).astype(BF16)
     relative = ids[...] - me
     relative = jnp.where(relative < 0, relative + experts, relative)
-    onehot = relative == lax.broadcasted_iota(jnp.int32, (rows, experts), 1)
+    onehot = relative == lax.broadcasted_iota(jnp.int32, (experts, rows), 0)
     onehot = jnp.where(onehot, 1.0, 0.0)
     r_i = lax.broadcasted_iota(jnp.int32, (rows, rows), 0)
     c_i = lax.broadcasted_iota(jnp.int32, (rows, rows), 1)
-    below = jnp.where(c_i < r_i, 1.0, 0.0).astype(BF16)
-    earlier = jnp.dot(below, onehot.astype(BF16), preferred_element_type=F32)
-    slot = jnp.sum(earlier * onehot, axis=1, keepdims=True)
+    above = jnp.where(r_i < c_i, 1.0, 0.0).astype(BF16)
+    earlier = jnp.dot(onehot.astype(BF16), above, preferred_element_type=F32)
+    slot = jnp.sum(earlier * onehot, axis=0, keepdims=True)
     target = relative.astype(F32) * CAP + slot
-    placed_t = jnp.where(
-        target == lax.broadcasted_iota(jnp.int32, (rows, slots), 1).astype(F32), 1.0, 0.0
+    placed = jnp.where(
+        target == lax.broadcasted_iota(jnp.int32, (slots, rows), 0).astype(F32), 1.0, 0.0
     ).astype(BF16)
     spread = jnp.where(r_i == c_i, target, 0.0).astype(BF16)
-    target_rows = jnp.dot(jnp.ones((slots, rows), BF16), spread, preferred_element_type=F32)
-    placed = jnp.where(
-        target_rows == lax.broadcasted_iota(jnp.int32, (slots, rows), 0).astype(F32), 1.0, 0.0
+    target_cols = jnp.dot(spread, jnp.ones((rows, slots), BF16), preferred_element_type=F32)
+    placed_t = jnp.where(
+        target_cols == lax.broadcasted_iota(jnp.int32, (rows, slots), 1).astype(F32), 1.0, 0.0
     ).astype(BF16)
     out2d[...] = jnp.dot(placed, normed, preferred_element_type=F32).astype(BF16)
     for i in range(experts):
@@ -291,6 +291,17 @@
             give_back(c, i).wait_send()
 
 
+def finish_kernel(mixed_in, att_in, mixed, att, sem):
+    copies = [
+        pltpu.make_async_copy(mixed_in, mixed, sem.at[0]),
+        pltpu.make_async_copy(att_in, att, sem.at[1]),
+    ]
+    for copy in copies:
+        copy.start()
+    for copy in copies:
+        copy.wait()
+
+
 def shards(tokens, norm_gain, expert_ids, w_in, w_out, queries, keys, values, new_keys, new_values, lens):
     experts = lax.axis_size("expert")
     rows, width = tokens.shape
@@ -301,22 +312,23 @@
     ctx = keys.shape[1]
     piece = half // RETURN_PIECES
     dma = pltpu.SemaphoreType.DMA
-    gain = norm_gain.reshape(1, width)
-    any_spec = pl.BlockSpec(memory_space=pl.ANY)
+    ids = expert_ids.reshape(1, rows)
+    hbm = pl.BlockSpec(memory_space=pltpu.HBM)
     vmem = pl.BlockSpec(memory_space=pltpu.VMEM)
     like = lambda a: pltpu.VMEM(a.shape, a.dtype)
-    return pl.pallas_call(
-        functools.partial(step_kernel, experts),
-        out_shape=(
+    outs = (
             jax.ShapeDtypeStruct((rows, half), BF16),
             jax.ShapeDtypeStruct(queries.shape, BF16),
-        ),
-        in_specs=[pl.BlockSpec(memory_space=pltpu.SMEM)] + [any_spec] * 10,
+        )
+    mixed, att = pl.pallas_call(
+        functools.partial(step_kernel, experts),
+        out_shape=(pltpu.VMEM((rows, half), BF16), pltpu.VMEM(queries.shape, BF16)),
+        in_specs=[pl.BlockSpec(memory_space=pltpu.SMEM)] + [hbm] * 10,
         out_specs=(vmem, vmem),
         scratch_shapes=[
             like(tokens),
-            like(gain),
-            like(expert_ids),
+            like(norm_gain),
+            like(ids),
             pltpu.VMEM((2, half, inner), BF16),
             pltpu.VMEM((2, inner, half), BF16),
             like(queries),
@@ -356,7 +368,15 @@
         compiler_params=pltpu.CompilerParams(
             collective_id=0, has_side_effects=True, vmem_limit_bytes=60 * 1024 * 1024
         ),
-    )(lens, tokens, gain, expert_ids, w_in, w_out, queries, keys, values, new_keys, new_values)
+    )(lens, tokens, norm_gain, ids, w_in, w_out, queries, keys, values, new_keys, new_values)
+    return pl.pallas_call(
+        finish_kernel,
+        out_shape=outs,
+        in_specs=[vmem, vmem],
+        out_specs=(hbm, hbm),
+        scratch_shapes=[dma((2,))],
+        compiler_params=pltpu.CompilerParams(vmem_limit_bytes=1024 * 1024),
+    )(mixed, att)
 
 
 def solution(mesh):

time: 31.5 us -> 25.9 us (0.82)
  local copies, waits for them, and re-layouts: 5.49 us -> 0 us
    unnamed x3 -> x0, local copies, waits for them, and re-layouts: 4.18 us -> none
    reshape x1 -> x0, local copies, waits for them, and re-layouts: 1.31 us -> none  [shards(): gain = norm_gain.reshape(1, width)]
    pallas_call x1 -> x2, Pallas kernels: 25.1 us -> 25.1 us  [the longest x1 24.4 us: shards(): pl.pallas_call(functools.partial(step_kernel, experts), out_shape=(pltpu....]
where the time goes in v2:
time: 25.9 us; the launch traced here: 25.7 us
  Pallas kernels  25.1 us (97%)
  between operations  0.64 us (2%)
    pallas_call x1, Pallas kernels, shards(): pl.pallas_call(functools.partial(step_kernel, experts), out_shape=(pltpu....  24.4 us
    pallas_call x1, Pallas kernels, shards(): pl.pallas_call(finish_kernel, out_shape=outs, in_specs=[vmem, vmem], out_...  0.66 us

profile of v2, /device:TPU:0, one launch (start us, length us, event | category | flops | bytes accessed | tf_op | source)
XLA Modules:
  0.0 25.7 jit_solution(7268931269041263452)
XLA Ops:
  0.6 24.4 %shard_map.122 = (bf16[16,2048]{1,0:T(8,128)(2,1)S(1)}, bf16[16,1024]{1,0:T(8,128)(2,1)S(1)}) custom-call(s32[16]{0:T(128)} %lens.1, bf16[16,4096]{1,0:T(8,128)(2,1)} %tok_h.1, bf16[4096]{0:T(1024)(128)(2,1)} %gain_h.1, s32[1,16]{1,0:T(1,128)} %bitcast.1, bf16[1,4096,1024]{2,1,0:T(8,128)(2,1)} %win_h.1, bf16[1,1024,4096]{2,1,0:T(8,128)(2,1)} %wout_h.1, ...), custom_call_target="tpu_custom_call" | custom-call | tf_op jit(solution)/shard_map/pallas_call | solution.py:323
  25.1 0.7 %shard_map.123 = (bf16[16,2048]{1,0:T(8,128)(2,1)}, bf16[16,1024]{1,0:T(8,128)(2,1)}) custom-call(bf16[16,2048]{1,0:T(8,128)(2,1)S(1)} %get-tuple-element.4.mixed_in, bf16[16,1024]{1,0:T(8,128)(2,1)S(1)} %get-tuple-element.5.att_in), custom_call_target="tpu_custom_call" | custom-call | tf_op jit(solution)/shard_map/pallas_call | solution.py:372

commit v3 on v2

--- a/solution.py
+++ b/solution.py
@@ -13,6 +13,16 @@
 F32 = jnp.float32
 BF16 = jnp.bfloat16
 MESH = pl.DeviceIdType.MESH
+
+
+def partner(me, i):
+    bit = 1
+    at = me
+    while bit <= i:
+        if i & bit:
+            at = at + bit - 2 * bit * (me // bit % 2)
+        bit *= 2
+    return at
 
 
 def step_kernel(
@@ -77,6 +87,7 @@
     own_off = pl.multiple_of(core * half, half)
     other_off = pl.multiple_of(other * half, half)
     slots = experts * CAP
+    far_first = range(experts - 1, 0, -1)
 
     loads = [
         pltpu.make_async_copy(src, dst, load_sem.at[n])
@@ -101,9 +112,9 @@
         load.start()
 
     barrier = pltpu.get_barrier_semaphore()
-    for i in range(1, experts):
+    for i in far_first:
         pl.semaphore_signal(
-            barrier, inc=1, device_id=(lax.rem(me + i, experts), core), device_id_type=MESH
+            barrier, inc=1, device_id=(partner(me, i), core), device_id_type=MESH
         )
     pl.semaphore_signal(barrier, inc=1, device_id=(me, other), device_id_type=MESH)
     for load in loads[3:]:
@@ -115,8 +126,7 @@
     inverse = lax.rsqrt(jnp.mean(whole * whole, axis=-1, keepdims=True) + 1e-05)
     mine = tok[:, pl.ds(own_off, half)].astype(F32)
     normed = (mine * inverse * gain[pl.ds(own_off, half)].astype(F32)[None, :]).astype(BF16)
-    relative = ids[...] - me
-    relative = jnp.where(relative < 0, relative + experts, relative)
+    relative = jnp.bitwise_xor(ids[...], me)
     onehot = relative == lax.broadcasted_iota(jnp.int32, (experts, rows), 0)
     onehot = jnp.where(onehot, 1.0, 0.0)
     r_i = lax.broadcasted_iota(jnp.int32, (rows, rows), 0)
@@ -155,11 +165,11 @@
             dst_ref=arrived.at[i],
             send_sem=send_sem.at[i],
             recv_sem=recv_sem.at[i],
-            device_id=(lax.rem(me + i, experts), core),
+            device_id=(partner(me, i), core),
             device_id_type=MESH,
         )
 
-    for i in range(1, experts):
+    for i in far_first:
         send(i).start()
     relay(0).start()
     x_own[0:CAP, :] = out2d[0:CAP, :]
@@ -246,7 +256,7 @@
             dst_ref=back.at[c, i],
             send_sem=ret_send.at[c, i],
             recv_sem=ret_recv.at[c, i],
-            device_id=(lax.rem(me + experts - i, experts), core),
+            device_id=(partner(me, i), core),
             device_id_type=MESH,
         )
 
@@ -262,7 +272,7 @@
         own_part = jnp.dot(hidden, wout[1, :, cols], preferred_element_type=F32)
         part_copy(c).wait_recv()
         ret2d[c] = (own_part + part_recv[c].astype(F32)).astype(BF16)
-        for i in range(1, experts):
+        for i in far_first:
             ret[c, i] = ret2d[c, CAP * i : CAP * (i + 1), :]
             give_back(c, i).start()
         back2d[0:CAP, cols] = ret2d[c, 0:CAP, :]

time: 25.9 us -> 24.8 us (0.958)
  Pallas kernels: 25.1 us -> 24 us
    pallas_call x1, Pallas kernels: 24.4 us -> 23.3 us  [shards(): pl.pallas_call(functools.partial(step_kernel, experts), out_shape=(pltpu....]
where the time goes in v3:
time: 24.8 us; the launch traced here: 24.6 us
  Pallas kernels  24 us (97%)
  between operations  0.64 us (3%)
    pallas_call x1, Pallas kernels, shards(): pl.pallas_call(functools.partial(step_kernel, experts), out_shape=(pltpu....  23.3 us
    pallas_call x1, Pallas kernels, shards(): pl.pallas_call(finish_kernel, out_shape=outs, in_specs=[vmem, vmem], out_...  0.66 us

profile of v3, /device:TPU:0, one launch (start us, length us, event | category | flops | bytes accessed | tf_op | source)
XLA Modules:
  0.0 24.6 jit_solution(539656910410282536)
XLA Ops:
  0.6 23.3 %shard_map.122 = (bf16[16,2048]{1,0:T(8,128)(2,1)S(1)}, bf16[16,1024]{1,0:T(8,128)(2,1)S(1)}) custom-call(s32[16]{0:T(128)} %lens.1, bf16[16,4096]{1,0:T(8,128)(2,1)} %tok_h.1, bf16[4096]{0:T(1024)(128)(2,1)} %gain_h.1, s32[1,16]{1,0:T(1,128)} %bitcast.1, bf16[1,4096,1024]{2,1,0:T(8,128)(2,1)} %win_h.1, bf16[1,1024,4096]{2,1,0:T(8,128)(2,1)} %wout_h.1, ...), custom_call_target="tpu_custom_call" | custom-call | tf_op jit(solution)/shard_map/pallas_call | solution.py:333
  23.9 0.7 %shard_map.123 = (bf16[16,2048]{1,0:T(8,128)(2,1)}, bf16[16,1024]{1,0:T(8,128)(2,1)}) custom-call(bf16[16,2048]{1,0:T(8,128)(2,1)S(1)} %get-tuple-element.4.mixed_in, bf16[16,1024]{1,0:T(8,128)(2,1)S(1)} %get-tuple-element.5.att_in), custom_call_target="tpu_custom_call" | custom-call | tf_op jit(solution)/shard_map/pallas_call | solution.py:382

commit v4 on v3

--- a/solution.py
+++ b/solution.py
@@ -9,7 +9,8 @@
 
 HEAD = 128
 CAP = 2
-RETURN_PIECES = 2
+RETURN_PIECES = 1
+PART_PIECES = 2
 F32 = jnp.float32
 BF16 = jnp.bfloat16
 MESH = pl.DeviceIdType.MESH
@@ -227,6 +228,7 @@
     for i in range(1, experts):
         send(i).wait_recv()
         relay(i).start()
+    for i in range(1, experts):
         x_own[CAP * i : CAP * (i + 1), :] = arrived[i]
     loads[8].wait()
     hidden_part[...] = jnp.dot(x_own[...], win[0], preferred_element_type=F32)
@@ -239,6 +241,7 @@
     ).astype(BF16)
 
     piece = half // RETURN_PIECES
+    part = half // PART_PIECES
 
     def part_copy(c):
         return pltpu.make_async_remote_copy(
@@ -261,21 +264,21 @@
         )
 
     loads[10].wait()
-    for c in range(RETURN_PIECES):
+    for c in range(PART_PIECES):
         part_send[c] = jnp.dot(
-            hidden, wout[0, :, c * piece : (c + 1) * piece], preferred_element_type=F32
+            hidden, wout[0, :, c * part : (c + 1) * part], preferred_element_type=F32
         ).astype(BF16)
         part_copy(c).start()
     loads[11].wait()
-    for c in range(RETURN_PIECES):
-        cols = slice(c * piece, (c + 1) * piece)
+    for c in range(PART_PIECES):
+        cols = slice(c * part, (c + 1) * part)
         own_part = jnp.dot(hidden, wout[1, :, cols], preferred_element_type=F32)
         part_copy(c).wait_recv()
-        ret2d[c] = (own_part + part_recv[c].astype(F32)).astype(BF16)
-        for i in far_first:
-            ret[c, i] = ret2d[c, CAP * i : CAP * (i + 1), :]
-            give_back(c, i).start()
-        back2d[0:CAP, cols] = ret2d[c, 0:CAP, :]
+        ret2d[0, :, cols] = (own_part + part_recv[c].astype(F32)).astype(BF16)
+    for i in far_first:
+        ret[0, i] = ret2d[0, CAP * i : CAP * (i + 1), :]
+        give_back(0, i).start()
+    back2d[0:CAP, :] = ret2d[0, 0:CAP, :]
 
     loads[7].wait()
     attend_values(0, rows)
@@ -295,8 +298,9 @@
         send(i).wait_send()
     for i in range(experts):
         relay(i).wait_send()
+    for c in range(PART_PIECES):
+        part_copy(c).wait_send()
     for c in range(RETURN_PIECES):
-        part_copy(c).wait_send()
         for i in range(1, experts):
             give_back(c, i).wait_send()
 
@@ -353,8 +357,8 @@
             pltpu.VMEM((slots, half), BF16),
             pltpu.VMEM((slots, half), BF16),
             pltpu.VMEM((slots, inner), F32),
-            pltpu.VMEM((RETURN_PIECES, slots, piece), BF16),
-            pltpu.VMEM((RETURN_PIECES, slots, piece), BF16),
+            pltpu.VMEM((PART_PIECES, slots, half // PART_PIECES), BF16),
+            pltpu.VMEM((PART_PIECES, slots, half // PART_PIECES), BF16),
             pltpu.VMEM((RETURN_PIECES, slots, piece), BF16),
             pltpu.VMEM((RETURN_PIECES, experts, CAP, piece), BF16),
             pltpu.VMEM((RETURN_PIECES, experts, CAP, piece), BF16),
@@ -370,8 +374,8 @@
             dma((experts,)),
             dma((experts,)),
             dma((experts,)),
-            dma((RETURN_PIECES,)),
-            dma((RETURN_PIECES,)),
+            dma((PART_PIECES,)),
+            dma((PART_PIECES,)),
             dma((RETURN_PIECES, experts)),
             dma((RETURN_PIECES, experts)),
         ],

time: 24.8 us -> 24.3 us (0.980)
  Pallas kernels: 24 us -> 23.5 us
    pallas_call x1, Pallas kernels: 23.3 us -> 22.9 us  [shards(): pl.pallas_call(functools.partial(step_kernel, experts), out_shape=(pltpu....]
where the time goes in v4:
time: 24.3 us; the launch traced here: 24.1 us
  Pallas kernels  23.5 us (97%)
  between operations  0.64 us (3%)
    pallas_call x1, Pallas kernels, shards(): pl.pallas_call(functools.partial(step_kernel, experts), out_shape=(pltpu....  22.9 us
    pallas_call x1, Pallas kernels, shards(): pl.pallas_call(finish_kernel, out_shape=outs, in_specs=[vmem, vmem], out_...  0.66 us

profile of v4, /device:TPU:0, one launch (start us, length us, event | category | flops | bytes accessed | tf_op | source)
XLA Modules:
  0.0 24.1 jit_solution(5389269666502896694)
XLA Ops:
  0.6 22.9 %shard_map.122 = (bf16[16,2048]{1,0:T(8,128)(2,1)S(1)}, bf16[16,1024]{1,0:T(8,128)(2,1)S(1)}) custom-call(s32[16]{0:T(128)} %lens.1, bf16[16,4096]{1,0:T(8,128)(2,1)} %tok_h.1, bf16[4096]{0:T(1024)(128)(2,1)} %gain_h.1, s32[1,16]{1,0:T(1,128)} %bitcast.1, bf16[1,4096,1024]{2,1,0:T(8,128)(2,1)} %win_h.1, bf16[1,1024,4096]{2,1,0:T(8,128)(2,1)} %wout_h.1, ...), custom_call_target="tpu_custom_call" | custom-call | tf_op jit(solution)/shard_map/pallas_call | solution.py:337
  23.5 0.7 %shard_map.123 = (bf16[16,2048]{1,0:T(8,128)(2,1)}, bf16[16,1024]{1,0:T(8,128)(2,1)}) custom-call(bf16[16,2048]{1,0:T(8,128)(2,1)S(1)} %get-tuple-element.4.mixed_in, bf16[16,1024]{1,0:T(8,128)(2,1)S(1)} %get-tuple-element.5.att_in), custom_call_target="tpu_custom_call" | custom-call | tf_op jit(solution)/shard_map/pallas_call | solution.py:386
